TPU v7x, 32 devices: a whole 2x2x4 slice. The times are simulated.
32 devices in a mesh: shard: 8 (over z, core), rep: 4 (over y, x).
Axes of the slice: x: 2, y: 2, z: 4, core: 2. Of those that a mesh axis runs over, the one named last changes fastest.
Arguments:
- tokens: bfloat16 [2, 8192, 1024], P(None, ('shard', 'rep')), may hold values from -6 to 6
- cotangent: bfloat16 [2, 8192, 1024], P(None, ('shard', 'rep')), may hold values from -6 to 6
- seq_lengths: int32 [2, 4, 8, 4], P(None, 'rep'), may hold values from 1 to 128, 256 in all within a row
- dealing: int32 [2, 4, 32], P(None, 'rep'), may hold values from 0 to 31, each once within a row
- attention_gain: bfloat16 [1024], P('shard'), may hold values from 0.25 to 1.75
- attention_shift: bfloat16 [1024], P('shard'), may hold values from -1 to 1
- input_weight: bfloat16 [1024, 3072], P('shard'), may hold values from -0.25 to 0.25
- query_bias: bfloat16 [1024], P('shard'), may hold values from -1 to 1
- value_bias: bfloat16 [1024], P('shard'), may hold values from -1 to 1
- output_weight: bfloat16 [1024, 1024], P('shard'), may hold values from -0.5 to 0.5
- output_bias: bfloat16 [1024], P('shard'), may hold values from -1 to 1
- feed_gain: bfloat16 [1024], P('shard'), may hold values from 0.25 to 1.75
- feed_shift: bfloat16 [1024], P('shard'), may hold values from -1 to 1
- up_weight: bfloat16 [1024, 4096], P('shard'), may hold values from -0.1875 to 0.1875
- up_bias: bfloat16 [4096], P('shard'), may hold values from -1 to 1
- down_weight: bfloat16 [4096, 1024], P('shard'), may hold values from -0.09375 to 0.09375
- down_bias: bfloat16 [1024], P('shard'), may hold values from -1 to 1
Outputs:
- block_out: bfloat16 [2, 8192, 1024], P(None, ('shard', 'rep'))
- input_grad: bfloat16 [2, 8192, 1024], P(None, ('shard', 'rep'))
- attention_gain_grad: float32 [1024], P('shard')
- attention_shift_grad: float32 [1024], P('shard')
- input_weight_grad: float32 [1024, 3072], P('shard')
- query_bias_grad: float32 [1024], P('shard')
- value_bias_grad: float32 [1024], P('shard')
- output_weight_grad: float32 [1024, 1024], P('shard')
- output_bias_grad: float32 [1024], P('shard')
- feed_gain_grad: float32 [1024], P('shard')
- feed_shift_grad: float32 [1024], P('shard')
- up_weight_grad: float32 [1024, 4096], P('shard')
- up_bias_grad: float32 [4096], P('shard')
- down_weight_grad: float32 [4096, 1024], P('shard')
- down_bias_grad: float32 [1024], P('shard')
Inputs may be any that keep to these rules, and one draw needn't show every extreme that they name: `seq_lengths`: for every micro-batch and replica, the 4 lengths given for each index of shard add up to 256. `dealing`: for every micro-batch and replica, each dealt number appears once; number n goes to index n // 4 of shard.
All inputs are finite; a program needn't handle non-finite values.
Results may differ from a plain program's by a relative error of at most 0.013.
The roundings to bfloat16 on the way count: a program that leaves them out, or rounds other values in their place, can miss the bound.
Values may be sent and summed in bfloat16 or wider, within the bound.
A program may use at most 256 MiB of HBM per device.

v0:
```python
from functools import partial
import jax
import jax.numpy as jnp
from jax import lax
from jax.sharding import PartitionSpec as P

HD = 64
EPSILON = 1e-05
MASKED = -1e30


def deal_maps(seq_lengths, dealing, rows_dev):
    groups, per_device = seq_lengths.shape
    total_seqs = groups * per_device
    numbers = jnp.arange(total_seqs, dtype=jnp.int32)
    flat_lengths = seq_lengths.reshape(total_seqs)
    matched = (dealing[:, None] == numbers[None, :]).astype(jnp.int32)
    packed_length = jnp.sum(matched * flat_lengths[None, :], axis=1, dtype=jnp.int32)
    packed_start = jnp.cumsum(packed_length, dtype=jnp.int32) - packed_length
    start_of = jnp.sum(matched * packed_start[:, None], axis=0, dtype=jnp.int32).reshape(
        groups, per_device
    )
    bin_start = jnp.cumsum(seq_lengths, axis=1, dtype=jnp.int32) - seq_lengths
    places = jnp.arange(rows_dev, dtype=jnp.int32)
    inside = (places[None, :, None] >= bin_start[:, None, :]).astype(jnp.int32)
    segment = jnp.sum(inside, axis=2, dtype=jnp.int32) - 1
    picked = (segment[:, :, None] == jnp.arange(per_device, dtype=jnp.int32)[None, None, :]).astype(
        jnp.int32
    )
    position = places[None, :] - jnp.sum(picked * bin_start[:, None, :], axis=2, dtype=jnp.int32)
    source = jnp.sum(picked * start_of[:, None, :], axis=2, dtype=jnp.int32) + position
    total_rows = groups * rows_dev
    all_rows = jnp.arange(total_rows, dtype=jnp.int32)
    owner_seq = (
        jnp.sum(
            (all_rows[:, None] >= packed_start[None, :]).astype(jnp.int32), axis=1, dtype=jnp.int32
        )
        - 1
    )
    owner_hit = (owner_seq[:, None] == numbers[None, :]).astype(jnp.int32)
    offset = all_rows - jnp.sum(owner_hit * packed_start[None, :], axis=1, dtype=jnp.int32)
    target = jnp.sum(owner_hit * dealing[None, :], axis=1, dtype=jnp.int32)
    target_hit = (target[:, None] == numbers[None, :]).astype(jnp.int32)
    flat_start = bin_start.reshape(total_seqs)
    backward_row = (
        target // per_device * rows_dev
        + jnp.sum(target_hit * flat_start[None, :], axis=1, dtype=jnp.int32)
        + offset
    )
    return (
        source.reshape(total_rows),
        segment.reshape(total_rows),
        position.reshape(total_rows),
        backward_row,
    )


def layer_norm(values, norm_gain, norm_shift):
    center = values - jnp.mean(values, axis=-1, keepdims=True)
    spread = jnp.mean(center * center, axis=-1, keepdims=True)
    return center * lax.rsqrt(spread + EPSILON) * norm_gain + norm_shift


def gelu_tanh(values):
    return jax.nn.gelu(values, approximate=True)


def rows_dot(left, right):
    return lax.dot_general(
        left, right, (((0,), (0,)), ((), ())), preferred_element_type=jnp.float32
    )


def back_dot(left, right):
    return lax.dot_general(
        left, right, (((1,), (1,)), ((), ())), preferred_element_type=jnp.float32
    )


def column_sum(values):
    return jnp.sum(values.astype(jnp.float32), axis=0)


def attention_scores(queries, keys_all, allowed):
    raw_scores = jnp.einsum("qhd,khd->hqk", queries, keys_all, preferred_element_type=jnp.float32)
    return jnp.where(allowed[None], raw_scores * float(HD) ** (-0.5), MASKED)


def take_rows(wanted, carried, pieces):
    row_count = pieces[0].shape[1]
    present = (wanted >= 0) & (wanted < row_count)
    clipped = jnp.clip(wanted, 0, row_count - 1)[:, :, None]
    return tuple(
        (
            jnp.where(
                present[:, :, None], jnp.take_along_axis(shard_rows, clipped, axis=1), previous
            )
            for shard_rows, previous in zip(pieces, carried)
        )
    )


def forward_rows(token_rows, segment, position, weights):
    (
        attention_gain,
        attention_shift,
        input_weight,
        query_bias,
        value_bias,
        output_weight,
        output_bias,
        feed_gain,
        feed_shift,
        up_weight,
        up_bias,
        down_weight,
        down_bias,
    ) = weights
    width = token_rows.shape[1]
    heads = width // HD
    inputs = token_rows.astype(jnp.float32)
    normed, first_back = jax.vjp(
        layer_norm, inputs, attention_gain.astype(jnp.float32), attention_shift.astype(jnp.float32)
    )
    normed_low = normed.astype(jnp.bfloat16)
    mixed = jnp.dot(normed_low, input_weight, preferred_element_type=jnp.float32)
    queries = (
        (mixed[:, :width] + query_bias.astype(jnp.float32))
        .astype(jnp.bfloat16)
        .reshape(-1, heads, HD)
    )
    keys_all = mixed[:, width : 2 * width].astype(jnp.bfloat16).reshape(-1, heads, HD)
    values_all = (
        (mixed[:, 2 * width :] + value_bias.astype(jnp.float32))
        .astype(jnp.bfloat16)
        .reshape(-1, heads, HD)
    )
    allowed = (segment[:, None] == segment[None, :]) & (position[None, :] <= position[:, None])
    scores = attention_scores(queries, keys_all, allowed)
    log_total = jax.nn.logsumexp(scores, axis=-1, keepdims=True)
    soft_low = jnp.exp(scores - log_total).astype(jnp.bfloat16)
    attended = jnp.einsum(
        "hqk,khd->qhd", soft_low, values_all, preferred_element_type=jnp.float32
    ).reshape(-1, width)
    branch = attended.astype(jnp.bfloat16)
    middle = (
        inputs
        + jnp.dot(branch, output_weight, preferred_element_type=jnp.float32)
        + output_bias.astype(jnp.float32)
    )
    normed_two, second_back = jax.vjp(
        layer_norm, middle, feed_gain.astype(jnp.float32), feed_shift.astype(jnp.float32)
    )
    normed_two_low = normed_two.astype(jnp.bfloat16)
    hidden = jnp.dot(
        normed_two_low, up_weight, preferred_element_type=jnp.float32
    ) + up_bias.astype(jnp.float32)
    activated, gelu_back = jax.vjp(gelu_tanh, hidden)
    activated_low = activated.astype(jnp.bfloat16)
    result = (
        middle
        + jnp.dot(activated_low, down_weight, preferred_element_type=jnp.float32)
        + down_bias.astype(jnp.float32)
    )
    saved_state = (
        normed_low,
        queries,
        keys_all,
        values_all,
        allowed,
        log_total,
        branch,
        normed_two_low,
        activated_low,
        first_back,
        second_back,
        gelu_back,
    )
    return (result.astype(jnp.bfloat16), saved_state)


def backward_rows(cotangent_rows, saved_state, matrices):
    input_weight, output_weight, up_weight, down_weight = matrices
    (
        normed_low,
        queries,
        keys_all,
        values_all,
        allowed,
        log_total,
        branch,
        normed_two_low,
        activated_low,
        first_back,
        second_back,
        gelu_back,
    ) = saved_state
    width = branch.shape[1]
    heads = width // HD
    score_scale = float(HD) ** (-0.5)
    upstream = cotangent_rows.astype(jnp.float32)
    down_low = upstream.astype(jnp.bfloat16)
    down_weight_grad = rows_dot(activated_low, down_low)
    down_bias_grad = column_sum(down_low)
    (hidden_grad,) = gelu_back(back_dot(down_low, down_weight))
    hidden_low = hidden_grad.astype(jnp.bfloat16)
    up_weight_grad = rows_dot(normed_two_low, hidden_low)
    up_bias_grad = column_sum(hidden_low)
    feed_part, feed_gain_grad, feed_shift_grad = second_back(back_dot(hidden_low, up_weight))
    middle_grad = upstream + feed_part
    output_low = middle_grad.astype(jnp.bfloat16)
    output_weight_grad = rows_dot(branch, output_low)
    output_bias_grad = column_sum(output_low)
    attended_low = back_dot(output_low, output_weight).astype(jnp.bfloat16).reshape(-1, heads, HD)
    scores = attention_scores(queries, keys_all, allowed)
    soft = jnp.exp(scores - log_total)
    soft_grad = jnp.einsum(
        "qhd,khd->hqk", attended_low, values_all, preferred_element_type=jnp.float32
    )
    score_low = (soft * (soft_grad - jnp.sum(soft * soft_grad, axis=-1, keepdims=True))).astype(
        jnp.bfloat16
    )
    query_grad = (
        (
            jnp.einsum("hqk,khd->qhd", score_low, keys_all, preferred_element_type=jnp.float32)
            * score_scale
        )
        .astype(jnp.bfloat16)
        .reshape(-1, width)
    )
    key_grad = (
        (
            jnp.einsum("hqk,qhd->khd", score_low, queries, preferred_element_type=jnp.float32)
            * score_scale
        )
        .astype(jnp.bfloat16)
        .reshape(-1, width)
    )
    value_grad = (
        jnp.einsum(
            "hqk,qhd->khd",
            soft.astype(jnp.bfloat16),
            attended_low,
            preferred_element_type=jnp.float32,
        )
        .astype(jnp.bfloat16)
        .reshape(-1, width)
    )
    mixed_grad = jnp.concatenate([query_grad, key_grad, value_grad], axis=1)
    input_weight_grad = rows_dot(normed_low, mixed_grad)
    inputs_part, attention_gain_grad, attention_shift_grad = first_back(
        back_dot(mixed_grad, input_weight)
    )
    input_grad = (middle_grad + inputs_part).astype(jnp.bfloat16)
    return (
        input_grad,
        (
            attention_gain_grad,
            attention_shift_grad,
            input_weight_grad,
            column_sum(query_grad),
            column_sum(value_grad),
            output_weight_grad,
            output_bias_grad,
            feed_gain_grad,
            feed_shift_grad,
            up_weight_grad,
            up_bias_grad,
            down_weight_grad,
            down_bias_grad,
        ),
    )


def shards(
    tokens,
    cotangent,
    seq_lengths,
    dealing,
    attention_gain,
    attention_shift,
    input_weight,
    query_bias,
    value_bias,
    output_weight,
    output_bias,
    feed_gain,
    feed_shift,
    up_weight,
    up_bias,
    down_weight,
    down_bias,
):
    micro_count, tok_rows, width = tokens.shape
    own_start = lax.axis_index("shard") * tok_rows
    full_maps = jax.vmap(partial(deal_maps, rows_dev=tok_rows))(seq_lengths[:, 0], dealing[:, 0])
    source, segment, position, backward_row = [
        lax.dynamic_slice_in_dim(member, own_start, tok_rows, 1) for member in full_maps
    ]
    empty_rows = jnp.zeros_like(tokens)
    dealt_tokens, dealt_cotangent = take_rows(
        source,
        (empty_rows, empty_rows),
        (
            lax.all_gather(tokens, "shard", axis=1, tiled=True),
            lax.all_gather(cotangent, "shard", axis=1, tiled=True),
        ),
    )
    weights = (
        attention_gain,
        attention_shift,
        input_weight,
        query_bias,
        value_bias,
        output_weight,
        output_bias,
        feed_gain,
        feed_shift,
        up_weight,
        up_bias,
        down_weight,
        down_bias,
    )
    totals = None
    results = []
    input_grads = []
    for micro_step in range(micro_count):
        forward_weights = (
            lax.all_gather(weights[0], "shard", axis=0, tiled=True),
            lax.all_gather(weights[1], "shard", axis=0, tiled=True),
            lax.all_gather(weights[2], "shard", axis=0, tiled=True),
            lax.all_gather(weights[3], "shard", axis=0, tiled=True),
            lax.all_gather(weights[4], "shard", axis=0, tiled=True),
            lax.all_gather(weights[5], "shard", axis=0, tiled=True),
            lax.all_gather(weights[6], "shard", axis=0, tiled=True),
            lax.all_gather(weights[7], "shard", axis=0, tiled=True),
            lax.all_gather(weights[8], "shard", axis=0, tiled=True),
            lax.all_gather(weights[9], "shard", axis=0, tiled=True),
            lax.all_gather(weights[10], "shard", axis=0, tiled=True),
            lax.all_gather(weights[11], "shard", axis=0, tiled=True),
            lax.all_gather(weights[12], "shard", axis=0, tiled=True),
        )
        result, saved_state = forward_rows(
            dealt_tokens[micro_step], segment[micro_step], position[micro_step], forward_weights
        )
        matrices = (
            lax.all_gather(input_weight, "shard", axis=0, tiled=True),
            lax.all_gather(output_weight, "shard", axis=0, tiled=True),
            lax.all_gather(up_weight, "shard", axis=0, tiled=True),
            lax.all_gather(down_weight, "shard", axis=0, tiled=True),
        )
        input_grad, local_grads = backward_rows(dealt_cotangent[micro_step], saved_state, matrices)
        results.append(result)
        input_grads.append(input_grad)
        if micro_step == 0:
            totals = local_grads
        else:
            totals = tuple((earlier + latest for earlier, latest in zip(totals, local_grads)))
    totals = lax.psum_scatter(totals, "shard", scatter_dimension=0, tiled=True)
    totals = lax.psum(totals, "rep")
    restored_out, restored_grad = take_rows(
        backward_row,
        (empty_rows, empty_rows),
        (
            lax.all_gather(jnp.stack(results), "shard", axis=1, tiled=True),
            lax.all_gather(jnp.stack(input_grads), "shard", axis=1, tiled=True),
        ),
    )
    return (restored_out, restored_grad) + tuple(totals)


def solution(mesh):
    return jax.shard_map(
        shards,
        mesh=mesh,
        in_specs=(
            P(None, ("shard", "rep"), None),
            P(None, ("shard", "rep"), None),
            P(None, "rep", None, None),
            P(None, "rep", None),
            P("shard"),
            P("shard"),
            P("shard", None),
            P("shard"),
            P("shard"),
            P("shard", None),
            P("shard"),
            P("shard"),
            P("shard"),
            P("shard", None),
            P("shard"),
            P("shard", None),
            P("shard"),
        ),
        out_specs=(
            P(None, ("shard", "rep"), None),
            P(None, ("shard", "rep"), None),
            P("shard"),
            P("shard"),
            P("shard", None),
            P("shard"),
            P("shard"),
            P("shard", None),
            P("shard"),
            P("shard"),
            P("shard"),
            P("shard", None),
            P("shard"),
            P("shard", None),
            P("shard"),
        ),
        check_vma=False,
    )
```

profile of v0, /device:TPU:0, one launch (start us, length us, event | category | flops | bytes accessed | tf_op | source)
XLA Modules:
  0.0 1307.6 jit_solution(15719994966998990020)
XLA Ops:
  11.6 13.5 %all-gather = bf16[8,1,128]{2,1,0:T(2,128)(2,1)S(1)} all-gather(bf16[1,1,128]{2,1,0:T(2,128)(2,1)S(1)} %bitcast.346), channel_id=1, replica_groups=mesh['shard'=8,'rep'=4] {'shard'}, dimensions={0}, use_global_device_ids=true | all-gather | bytes 2304 | tf_op jit(solution)/shard_map/all_gather | solution.py:329
  34.1 12.6 all-gather.3
  46.8 9.1 all-gather.2
  55.9 12.1 all-gather.4
  67.9 9.1 all-gather.5
  77.0 10.3 all-gather.6
  88.1 14.0 %all-gather.7 = bf16[8,1,512]{2,1,0:T(2,128)(2,1)S(1)} all-gather(bf16[1,1,512]{2,1,0:T(2,128)(2,1)S(1)} %reshape.473), channel_id=1, replica_groups=mesh['shard'=8,'rep'=4] {'shard'}, dimensions={0}, use_global_device_ids=true | all-gather | bytes 9216 | tf_op jit(solution)/shard_map/all_gather | solution.py:339
  112.8 64.0 %all-gather.18.cloned.1.call-done = bf16[2,2048,1024]{2,1,0:T(8,128)(2,1)} async-done(((bf16[2,256,1024]{2,1,0:T(8,128)(2,1)}), bf16[2,2048,1024]{2,1,0:T(8,128)(2,1)}) %all-gather.18.cloned.1.call-update) | async-done | bytes 8388624 | tf_op jit(solution)/shard_map/all_gather | solution.py:305
  176.8 11.2 gather_fusion
  191.2 50.5 %all-gather.20.cloned.1.call-done = bf16[1024,3072]{1,0:T(8,128)(2,1)} async-done(((bf16[128,3072]{1,0:T(8,128)(2,1)}), bf16[1024,3072]{1,0:T(8,128)(2,1)}) %all-gather.20.cloned.1.call-update) | async-done | bytes 6291472 | tf_op jit(solution)/shard_map/all_gather | solution.py:331
  279.5 74.3 %all-gather.24.cloned.1.call-done = bf16[1024,4096]{1,0:T(8,128)(2,1)} async-done(((bf16[128,4096]{1,0:T(8,128)(2,1)}), bf16[1024,4096]{1,0:T(8,128)(2,1)}) %all-gather.24.cloned.1.call-update) | async-done | bytes 8388624 | tf_op jit(solution)/shard_map/all_gather | solution.py:338
  366.6 69.2 %all-gather.26.cloned.1.call-done = bf16[4096,1024]{1,0:T(8,128)(2,1)} async-done(((bf16[512,1024]{1,0:T(8,128)(2,1)}), bf16[4096,1024]{1,0:T(8,128)(2,1)}) %all-gather.26.cloned.1.call-update) | async-done | bytes 8388624 | tf_op jit(solution)/shard_map/all_gather | solution.py:340
  507.3 11.0 fusion.65
  518.4 11.7 convolution_add_fusion
  534.6 10.1 convolution_add_fusion.1
  545.4 9.3 all-gather.8
  584.1 65.0 %reduce-scatter.5.cloned.1.call-done = f32[128,3072]{1,0:T(8,128)} async-done(((f32[1024,3072]{1,0:T(8,128)}), f32[128,3072]{1,0:T(8,128)}) %reduce-scatter.5.cloned.1.call-update) | async-done | bytes 1572880 | tf_op jit(solution)/shard_map/reduce_scatter | solution.py:359
  649.1 169.0 %reduce-scatter.11.cloned.1.call-done = f32[512,1024]{1,0:T(8,128)} async-done(((f32[4096,1024]{1,0:T(8,128)}), f32[512,1024]{1,0:T(8,128)}) %reduce-scatter.11.cloned.1.call-update) | async-done | bytes 2097168 | tf_op jit(solution)/shard_map/reduce_scatter | solution.py:359
  818.1 168.9 %reduce-scatter.9.cloned.1.call-done = f32[128,4096]{1,0:T(8,128)} async-done(((f32[1024,4096]{1,0:T(8,128)}), f32[128,4096]{1,0:T(8,128)}) %reduce-scatter.9.cloned.1.call-update) | async-done | bytes 2097168 | tf_op jit(solution)/shard_map/reduce_scatter | solution.py:359
  989.3 28.7 %all-reduce.9 = (f32[1024]{0:T(1024)S(1)}, f32[1024]{0:T(1024)S(1)}, f32[1024]{0:T(1024)S(1)}, f32[1024]{0:T(1024)S(1)}, f32[1024]{0:T(1024)S(1)}, /*index=5*/f3...) all-reduce(f32[1024]{0:T(1024)S(1)} %add.367, ...), channel_id=2, replica_groups=mesh['shard'=8,'rep'=4] {'shard'}, use_global_device_ids=true, to_apply=%region_35.37.clone | all-reduce | flops 12288 | bytes 98304
  1018.7 10.8 all-reduce.10
  1029.5 41.0 %all-gather.28.cloned.1.call-done = bf16[2,2048,1024]{2,1,0:T(8,128)(2,1)} async-done(((bf16[2,256,1024]{2,1,0:T(8,128)(2,1)}), bf16[2,2048,1024]{2,1,0:T(8,128)(2,1)}) %all-gather.28.cloned.1.call-update) | async-done | bytes 8388624 | tf_op jit(solution)/shard_map/all_gather | solution.py:365
  1078.6 74.4 %all-gather.32.cloned.1.call-done = bf16[2,2048,1024]{2,1,0:T(8,128)(2,1)} async-done(((bf16[2,256,1024]{2,1,0:T(8,128)(2,1)}), bf16[2,2048,1024]{2,1,0:T(8,128)(2,1)}) %all-gather.32.cloned.1.call-update) | async-done | bytes 8388624 | tf_op jit(solution)/shard_map/all_gather | solution.py:366
  1162.7 130.7 %all-reduce.14.cloned.1.call-done = (f32[128,3072]{1,0:T(8,128)}, f32[128,1024]{1,0:T(8,128)}, f32[128,4096]{1,0:T(8,128)}, f32[512,1024]{1,0:T(8,128)}) async-done(((f32[128,3072]{1,0:T(8,128)}, f32[128,1024]{1,0:T(8,128)}, f32[128,4096]{1,0:T(8,128)}, f32[512,1024]{1,0:T(8,128)}), (f32[128,3072]{1,0:T(8,128)}, f32[128,1024]{1,0:T(8,128)}, f32[128,4096]{1,0:T(8,128)}, ...) | async-done | bytes 6291472 | tf_op jit(solution)/shard_map/psum | solution.py:360
  (372 shorter events, 210.0 us)
Async XLA Ops:
  7.3 97.4 %all-gather.30.cloned.1.call-start = ((), (), s32[]{:S(2)}) async-start(), calls=%async_computation.10 | async-start | bytes 9437184 | tf_op jit(solution)/shard_map/all_gather | solution.py:306
  8.0 168.8 %all-gather.18.cloned.1.call-start = ((), (), s32[]{:S(2)}) async-start(), calls=%async_computation.4 | async-start | bytes 9437184 | tf_op jit(solution)/shard_map/all_gather | solution.py:305
  8.8 232.9 %all-gather.20.cloned.1.call-start = ((), (), s32[]{:S(2)}) async-start(), calls=%async_computation.5 | async-start | bytes 7077888 | tf_op jit(solution)/shard_map/all_gather | solution.py:331
  9.5 261.4 %all-gather.22.cloned.1.call-start = ((), (), s32[]{:S(2)}) async-start(), calls=%async_computation.6 | async-start | bytes 2359296 | tf_op jit(solution)/shard_map/all_gather | solution.py:334
  10.1 343.8 %all-gather.24.cloned.1.call-start = ((), (), s32[]{:S(2)}) async-start(), calls=%async_computation.7 | async-start | bytes 9437184 | tf_op jit(solution)/shard_map/all_gather | solution.py:338
  10.7 425.2 %all-gather.26.cloned.1.call-start = ((), (), s32[]{:S(2)}) async-start(), calls=%async_computation.8 | async-start | bytes 9437184 | tf_op jit(solution)/shard_map/all_gather | solution.py:340
  11.2 572.9 %reduce-scatter.7.cloned.1.call-start = ((), (), s32[]{:S(2)}) async-start(), calls=%async_computation.13 | async-start | bytes 4718592 | tf_op jit(solution)/shard_map/reduce_scatter | solution.py:359
  470.6 178.5 %reduce-scatter.5.cloned.1.call-start = ((), (), s32[]{:S(2)}) async-start(), calls=%async_computation.12 | async-start | bytes 14155776 | tf_op jit(solution)/shard_map/reduce_scatter | solution.py:359
  507.2 310.9 %reduce-scatter.11.cloned.1.call-start = ((), (), s32[]{:S(2)}) async-start(), calls=%async_computation.15 | async-start | bytes 18874368 | tf_op jit(solution)/shard_map/reduce_scatter | solution.py:359
  530.1 456.9 %reduce-scatter.9.cloned.1.call-start = ((), (), s32[]{:S(2)}) async-start(), calls=%async_computation.14 | async-start | bytes 18874368 | tf_op jit(solution)/shard_map/reduce_scatter | solution.py:359
  544.8 525.7 %all-gather.28.cloned.1.call-start = ((), (), s32[]{:S(2)}) async-start(), calls=%async_computation.9 | async-start | bytes 9437184 | tf_op jit(solution)/shard_map/all_gather | solution.py:365
  570.1 582.9 %all-gather.32.cloned.1.call-start = ((), (), s32[]{:S(2)}) async-start(), calls=%async_computation.11 | async-start | bytes 9437184 | tf_op jit(solution)/shard_map/all_gather | solution.py:366
  583.9 405.2 %copy-start.49 = (f32[16,64]{1,0:T(8,128)S(1)}, f32[16,64]{1,0:T(8,128)}, u32[]{:S(2)}) copy-start(f32[16,64]{1,0:T(8,128)} %get-tuple-element.121) | copy-start | bytes 12292
  583.9 405.3 %copy-start.57 = (f32[4096]{0:T(1024)S(1)}, f32[4096]{0:T(1024)}, u32[]{:S(2)}) copy-start(f32[4096]{0:T(1024)} %get-tuple-element.129) | copy-start | bytes 49156
  583.9 405.2 %copy-start.58 = (f32[4096]{0:T(1024)S(1)}, f32[4096]{0:T(1024)}, u32[]{:S(2)}) copy-start(f32[4096]{0:T(1024)} %get-tuple-element.131) | copy-start | bytes 49156
  583.9 405.2 %copy-start.78 = (f32[1024]{0:T(1024)S(1)}, f32[1024]{0:T(1024)}, u32[]{:S(2)}) copy-start(f32[1024]{0:T(1024)} %get-tuple-element.22) | copy-start | bytes 12292
  583.9 405.2 %copy-start.79 = (f32[1024]{0:T(1024)S(1)}, f32[1024]{0:T(1024)}, u32[]{:S(2)}) copy-start(f32[1024]{0:T(1024)} %get-tuple-element.102) | copy-start | bytes 12292
  583.9 405.3 %copy-start.76 = (f32[1024]{0:T(1024)S(1)}, f32[1024]{0:T(1024)}, u32[]{:S(2)}) copy-start(f32[1024]{0:T(1024)} %get-tuple-element.32) | copy-start | bytes 12292
  584.0 405.3 %copy-start.77 = (f32[1024]{0:T(1024)S(1)}, f32[1024]{0:T(1024)}, u32[]{:S(2)}) copy-start(f32[1024]{0:T(1024)} %get-tuple-element.100) | copy-start | bytes 12292
  584.0 405.3 %copy-start.61 = (f32[1024]{0:T(1024)S(1)}, f32[1024]{0:T(1024)}, u32[]{:S(2)}) copy-start(f32[1024]{0:T(1024)} %get-tuple-element.29) | copy-start | bytes 12292
  584.0 405.3 %copy-start.62 = (f32[1024]{0:T(1024)S(1)}, f32[1024]{0:T(1024)}, u32[]{:S(2)}) copy-start(f32[1024]{0:T(1024)} %get-tuple-element.30) | copy-start | bytes 12292
  584.0 405.3 %copy-start.59 = (f32[1024]{0:T(1024)S(1)}, f32[1024]{0:T(1024)}, u32[]{:S(2)}) copy-start(f32[1024]{0:T(1024)} %get-tuple-element.82) | copy-start | bytes 12292
  584.0 405.3 %copy-start.60 = (f32[1024]{0:T(1024)S(1)}, f32[1024]{0:T(1024)}, u32[]{:S(2)}) copy-start(f32[1024]{0:T(1024)} %get-tuple-element.84) | copy-start | bytes 12292
  584.0 709.4 %all-reduce.14.cloned.1.call-start = ((), (), s32[]{:S(2)}) async-start(), calls=%async_computation.16 | async-start | bytes 12582912 | tf_op jit(solution)/shard_map/psum | solution.py:360
  (82 other events, 4319.1 us)
Sparse Core Ops, SparseCore 0:
  9.7 84.8 all-gather.29
  96.2 80.5 all-gather.17
  178.4 63.1 all-gather.19
  243.1 27.7 all-gather.21
  272.4 81.4 all-gather.23
  355.3 80.5 all-gather.25
  470.7 48.3 reduce-scatter.6
  521.4 127.6 reduce-scatter.4
  651.5 166.6 reduce-scatter.10
  820.3 166.6 reduce-scatter.8
  989.2 81.2 all-gather.27
  1072.5 80.4 all-gather.31
  1156.7 136.6 all-reduce.13
where the time goes:
time: 1310 us
  waiting for transfers between devices  913 us (70%)
  matrix products  152 us (12%)
  blocking collectives  138 us (11%)
  local copies, waits for them, and re-layouts  63.7 us (5%)
  other arithmetic  22.4 us (2%)
  between operations  17 us (1%)
    reduce_scatter x4, waiting for transfers between devices, shards(): totals = lax.psum_scatter(totals, 'shard', scatter_dimension=0, tiled=True)  403 us
    psum x1, waiting for transfers between devices, shards(): totals = lax.psum(totals, 'rep')  131 us
    all_gather x1, waiting for transfers between devices, shards(): lax.all_gather(jnp.stack(input_grads), 'shard', axis=1, tiled=True)  74.4 us
    all_gather x1, waiting for transfers between devices, shards(): lax.all_gather(weights[9], 'shard', axis=0, tiled=True)  74.3 us
    all_gather x1, waiting for transfers between devices, shards(): lax.all_gather(weights[11], 'shard', axis=0, tiled=True)  69.2 us
    all_gather x1, waiting for transfers between devices, shards(): lax.all_gather(tokens, 'shard', axis=1, tiled=True)  64 us
    all_gather x1, waiting for transfers between devices, shards(): lax.all_gather(weights[2], 'shard', axis=0, tiled=True)  50.5 us
    dot_general x8, matrix products, rows_dot(): lax.dot_general(left, right, (((0,), (0,)), ((), ())), preferred_element_...  50 us
  transfers between devices with their start and end apart: 13, of which 11 were waited for; matrix products, arithmetic and copies ran while one was open for 14% of the time, Pallas kernels for 0%

commit v1 on v0

--- a/solution.py
+++ b/solution.py
@@ -7,6 +7,22 @@
 HD = 64
 EPSILON = 1e-05
 MASKED = -1e30
+
+
+def collect(x, axis, dim):
+    ways, here, lap = (lax.axis_size(axis), lax.axis_index(axis), x.shape[dim])
+    lengths = [n * ways if d == dim else n for d, n in enumerate(x.shape)]
+    full = lax.dynamic_update_slice_in_dim(jnp.zeros(lengths, x.dtype), x, here * lap, axis=dim)
+    going_up = going_down = x
+    for far in range(1, ways // 2 + 1):
+        going_up = lax.ppermute(going_up, axis, [(d, (d + 1) % ways) for d in range(ways)])
+        full = lax.dynamic_update_slice_in_dim(full, going_up, (here - far) % ways * lap, axis=dim)
+        if 2 * far < ways:
+            going_down = lax.ppermute(going_down, axis, [(d, (d - 1) % ways) for d in range(ways)])
+            full = lax.dynamic_update_slice_in_dim(
+                full, going_down, (here + far) % ways * lap, axis=dim
+            )
+    return full
 
 
 def deal_maps(seq_lengths, dealing, rows_dev):
@@ -362,7 +378,7 @@
         backward_row,
         (empty_rows, empty_rows),
         (
-            lax.all_gather(jnp.stack(results), "shard", axis=1, tiled=True),
+            collect(jnp.stack(results), "shard", 1),
             lax.all_gather(jnp.stack(input_grads), "shard", axis=1, tiled=True),
         ),
     )

time: 1310 us -> 1280 us (0.977)
  waiting for transfers between devices: 913 us -> 834 us
  local copies, waits for them, and re-layouts: 63.7 us -> 80.6 us
  starting transfers between devices: 0.73 us -> 15.9 us
    ppermute x0 -> x7, waiting for transfers between devices: none -> 104 us  [the longest x4 94.7 us: collect(): lax.ppermute(going_up, axis, [(d, (d + 1) % ways) for d in range(ways)])]
    psum x1, waiting for transfers between devices: 131 us -> 47.9 us  [shards(): totals = lax.psum(totals, 'rep')]
    all_gather x1, waiting for transfers between devices: 74.4 us -> 0.02 us  [shards(): lax.all_gather(jnp.stack(input_grads), 'shard', axis=1, tiled=True)]
    all_gather x1 -> x0, waiting for transfers between devices: 41 us -> none  [shards(): lax.all_gather(jnp.stack(results), 'shard', axis=1, tiled=True)]
    reduce_scatter x4, waiting for transfers between devices: 403 us -> 418 us  [shards(): totals = lax.psum_scatter(totals, 'shard', scatter_dimension=0, tiled=True)]
    ppermute x0 -> x7, starting transfers between devices: none -> 15.1 us  [the longest x3 10.9 us: collect(): lax.ppermute(going_down, axis, [(d, (d - 1) % ways) for d in range(ways)])]
  transfers between devices with their start and end apart: 13 -> 19, of which waited for: 11 -> 13; matrix products, arithmetic and copies ran while one was open for 14% -> 16% of each run, Pallas kernels for 0% -> 0%
where the time goes in v1:
time: 1280 us; the launch traced here: 1270 us
  waiting for transfers between devices  834 us (65%)
  matrix products  153 us (12%)
  blocking collectives  150 us (12%)
  local copies, waits for them, and re-layouts  80.6 us (6%)
  other arithmetic  22.4 us (2%)
  between operations  17.4 us (1%)
  starting transfers between devices  15.9 us (1%)
    reduce_scatter x4, waiting for transfers between devices, shards(): totals = lax.psum_scatter(totals, 'shard', scatter_dimension=0, tiled=True)  418 us
    ppermute x4, waiting for transfers between devices, collect(): lax.ppermute(going_up, axis, [(d, (d + 1) % ways) for d in range(ways)])  94.7 us
    all_gather x1, waiting for transfers between devices, shards(): lax.all_gather(weights[9], 'shard', axis=0, tiled=True)  74.3 us
    all_gather x1, waiting for transfers between devices, shards(): lax.all_gather(weights[11], 'shard', axis=0, tiled=True)  69.4 us
    all_gather x1, waiting for transfers between devices, shards(): lax.all_gather(tokens, 'shard', axis=1, tiled=True)  64 us
    all_gather x1, waiting for transfers between devices, shards(): lax.all_gather(weights[2], 'shard', axis=0, tiled=True)  50.5 us
    dot_general x8, matrix products, rows_dot(): lax.dot_general(left, right, (((0,), (0,)), ((), ())), preferred_element_...  49.9 us
    psum x1, waiting for transfers between devices, shards(): totals = lax.psum(totals, 'rep')  47.9 us
  transfers between devices with their start and end apart: 19, of which 13 were waited for; matrix products, arithmetic and copies ran while one was open for 16% of the time, Pallas kernels for 0%

profile of v1, /device:TPU:0, one launch (start us, length us, event | category | flops | bytes accessed | tf_op | source)
XLA Modules:
  0.0 1273.3 jit_solution(7219356738197048274)
XLA Ops:
  11.6 13.5 %all-gather = bf16[8,1,128]{2,1,0:T(2,128)(2,1)S(1)} all-gather(bf16[1,1,128]{2,1,0:T(2,128)(2,1)S(1)} %bitcast.346), channel_id=1, replica_groups=mesh['shard'=8,'rep'=4] {'shard'}, dimensions={0}, use_global_device_ids=true | all-gather | bytes 2304 | tf_op jit(solution)/shard_map/all_gather | solution.py:345
  34.1 12.6 all-gather.3
  55.9 12.1 all-gather.4
  67.9 9.1 all-gather.5
  77.0 10.3 all-gather.6
  88.1 14.0 %all-gather.7 = bf16[8,1,512]{2,1,0:T(2,128)(2,1)S(1)} all-gather(bf16[1,1,512]{2,1,0:T(2,128)(2,1)S(1)} %reshape.473), channel_id=1, replica_groups=mesh['shard'=8,'rep'=4] {'shard'}, dimensions={0}, use_global_device_ids=true | all-gather | bytes 9216 | tf_op jit(solution)/shard_map/all_gather | solution.py:355
  112.8 64.0 %all-gather.17.cloned.1.call-done = bf16[2,2048,1024]{2,1,0:T(8,128)(2,1)} async-done(((bf16[2,256,1024]{2,1,0:T(8,128)(2,1)}), bf16[2,2048,1024]{2,1,0:T(8,128)(2,1)}) %all-gather.17.cloned.1.call-update) | async-done | bytes 8388624 | tf_op jit(solution)/shard_map/all_gather | solution.py:321
  176.8 11.2 gather_fusion
  191.2 50.5 %all-gather.19.cloned.1.call-done = bf16[1024,3072]{1,0:T(8,128)(2,1)} async-done(((bf16[128,3072]{1,0:T(8,128)(2,1)}), bf16[1024,3072]{1,0:T(8,128)(2,1)}) %all-gather.19.cloned.1.call-update) | async-done | bytes 6291472 | tf_op jit(solution)/shard_map/all_gather | solution.py:347
  279.5 74.3 %all-gather.23.cloned.1.call-done = bf16[1024,4096]{1,0:T(8,128)(2,1)} async-done(((bf16[128,4096]{1,0:T(8,128)(2,1)}), bf16[1024,4096]{1,0:T(8,128)(2,1)}) %all-gather.23.cloned.1.call-update) | async-done | bytes 8388624 | tf_op jit(solution)/shard_map/all_gather | solution.py:354
  366.5 69.4 %all-gather.25.cloned.1.call-done = bf16[4096,1024]{1,0:T(8,128)(2,1)} async-done(((bf16[512,1024]{1,0:T(8,128)(2,1)}), bf16[4096,1024]{1,0:T(8,128)(2,1)}) %all-gather.25.cloned.1.call-update) | async-done | bytes 8388624 | tf_op jit(solution)/shard_map/all_gather | solution.py:356
  507.0 11.0 fusion.65
  518.0 11.8 convolution_add_fusion
  534.3 10.2 convolution_add_fusion.1
  559.5 9.1 all-gather.8
  568.6 80.4 %reduce-scatter.5.cloned.1.call-done = f32[128,3072]{1,0:T(8,128)} async-done(((f32[1024,3072]{1,0:T(8,128)}), f32[128,3072]{1,0:T(8,128)}) %reduce-scatter.5.cloned.1.call-update) | async-done | bytes 1572880 | tf_op jit(solution)/shard_map/reduce_scatter | solution.py:375
  649.0 169.0 %reduce-scatter.11.cloned.1.call-done = f32[512,1024]{1,0:T(8,128)} async-done(((f32[4096,1024]{1,0:T(8,128)}), f32[512,1024]{1,0:T(8,128)}) %reduce-scatter.11.cloned.1.call-update) | async-done | bytes 2097168 | tf_op jit(solution)/shard_map/reduce_scatter | solution.py:375
  818.0 168.9 %reduce-scatter.9.cloned.1.call-done = f32[128,4096]{1,0:T(8,128)} async-done(((f32[1024,4096]{1,0:T(8,128)}), f32[128,4096]{1,0:T(8,128)}) %reduce-scatter.9.cloned.1.call-update) | async-done | bytes 2097168 | tf_op jit(solution)/shard_map/reduce_scatter | solution.py:375
  1010.8 45.8 %collective-permute-done = bf16[2,256,1024]{2,1,0:T(8,128)(2,1)S(1)} collective-permute-done((bf16[2,256,1024]{2,1,0:T(8,128)(2,1)S(1)}, bf16[2,256,1024]{2,1,0:T(8,128)(2,1)S(1)}, u32[]{:S(2)}, u32[]{:S(2)}) %collective-permute-start) | collective-permute-done | bytes 1048608 | tf_op jit(solution)/shard_map/ppermute | solution.py:18
  1060.3 35.9 %collective-permute-done.2 = bf16[2,256,1024]{2,1,0:T(8,128)(2,1)} collective-permute-done((bf16[2,256,1024]{2,1,0:T(8,128)(2,1)S(1)}, bf16[2,256,1024]{2,1,0:T(8,128)(2,1)}, u32[]{:S(2)}, u32[]{:S(2)}) %collective-permute-start.2) | collective-permute-done | bytes 1048608 | tf_op jit(solution)/shard_map/ppermute | solution.py:18
  1111.0 13.0 %collective-permute-done.4 = bf16[2,256,1024]{2,1,0:T(8,128)(2,1)S(1)} collective-permute-done((bf16[2,256,1024]{2,1,0:T(8,128)(2,1)}, bf16[2,256,1024]{2,1,0:T(8,128)(2,1)S(1)}, u32[]{:S(2)}, u32[]{:S(2)}) %collective-permute-start.4) | collective-permute-done | bytes 1048608 | tf_op jit(solution)/shard_map/ppermute | solution.py:18
  1128.4 40.5 %all-reduce.9 = (f32[1024]{0:T(1024)S(1)}, f32[1024]{0:T(1024)S(1)}, f32[1024]{0:T(1024)S(1)}, f32[1024]{0:T(1024)S(1)}, f32[1024]{0:T(1024)S(1)}, /*index=5*/f3...) all-reduce(f32[1024]{0:T(1024)S(1)} %add.441, ...), channel_id=2, replica_groups=mesh['shard'=8,'rep'=4] {'shard'}, use_global_device_ids=true, to_apply=%region_35.37.clone | all-reduce | flops 12288 | bytes 98304
  1169.5 11.3 all-reduce.10
  1211.0 47.9 %all-reduce.14.cloned.1.call-done = (f32[128,3072]{1,0:T(8,128)}, f32[128,1024]{1,0:T(8,128)}, f32[128,4096]{1,0:T(8,128)}, f32[512,1024]{1,0:T(8,128)}) async-done(((f32[128,3072]{1,0:T(8,128)}, f32[128,1024]{1,0:T(8,128)}, f32[128,4096]{1,0:T(8,128)}, f32[512,1024]{1,0:T(8,128)}), (f32[128,3072]{1,0:T(8,128)}, f32[128,1024]{1,0:T(8,128)}, f32[128,4096]{1,0:T(8,128)}, ...) | async-done | bytes 6291472 | tf_op jit(solution)/shard_map/psum | solution.py:376
  (393 shorter events, 260.4 us)
Async XLA Ops:
  7.3 97.4 %all-gather.27.cloned.1.call-start = ((), (), s32[]{:S(2)}) async-start(), calls=%async_computation.9 | async-start | bytes 9437184 | tf_op jit(solution)/shard_map/all_gather | solution.py:322
  8.0 168.8 %all-gather.17.cloned.1.call-start = ((), (), s32[]{:S(2)}) async-start(), calls=%async_computation.4 | async-start | bytes 9437184 | tf_op jit(solution)/shard_map/all_gather | solution.py:321
  8.8 232.9 %all-gather.19.cloned.1.call-start = ((), (), s32[]{:S(2)}) async-start(), calls=%async_computation.5 | async-start | bytes 7077888 | tf_op jit(solution)/shard_map/all_gather | solution.py:347
  9.5 261.4 %all-gather.21.cloned.1.call-start = ((), (), s32[]{:S(2)}) async-start(), calls=%async_computation.6 | async-start | bytes 2359296 | tf_op jit(solution)/shard_map/all_gather | solution.py:350
  10.1 343.8 %all-gather.23.cloned.1.call-start = ((), (), s32[]{:S(2)}) async-start(), calls=%async_computation.7 | async-start | bytes 9437184 | tf_op jit(solution)/shard_map/all_gather | solution.py:354
  10.7 425.2 %all-gather.25.cloned.1.call-start = ((), (), s32[]{:S(2)}) async-start(), calls=%async_computation.8 | async-start | bytes 9437184 | tf_op jit(solution)/shard_map/all_gather | solution.py:356
  11.2 557.3 %reduce-scatter.7.cloned.1.call-start = ((), (), s32[]{:S(2)}) async-start(), calls=%async_computation.12 | async-start | bytes 4718592 | tf_op jit(solution)/shard_map/reduce_scatter | solution.py:375
  191.2 309.1 %copy-start.52 = (f32[256]{0:T(256)}, f32[256]{0:T(256)S(1)}, u32[]{:S(2)}) copy-start(f32[256]{0:T(256)S(1)} %fusion.79) | copy-start | bytes 3076
  273.4 190.9 %copy-start.49 = (f32[256]{0:T(256)}, f32[256]{0:T(256)S(1)}, u32[]{:S(2)}) copy-start(f32[256]{0:T(256)S(1)} %broadcast_multiply_fusion.2) | copy-start | bytes 3076
  279.2 185.1 %copy-start.54 = (f32[256]{0:T(256)}, f32[256]{0:T(256)S(1)}, u32[]{:S(2)}) copy-start(f32[256]{0:T(256)S(1)} %broadcast_multiply_fusion) | copy-start | bytes 3076
  279.5 184.8 %copy-start.55 = (f32[256]{0:T(256)}, f32[256]{0:T(256)S(1)}, u32[]{:S(2)}) copy-start(f32[256]{0:T(256)S(1)} %fusion.78) | copy-start | bytes 3076
  470.4 178.6 %reduce-scatter.5.cloned.1.call-start = ((), (), s32[]{:S(2)}) async-start(), calls=%async_computation.11 | async-start | bytes 14155776 | tf_op jit(solution)/shard_map/reduce_scatter | solution.py:375
  506.9 311.1 %reduce-scatter.11.cloned.1.call-start = ((), (), s32[]{:S(2)}) async-start(), calls=%async_computation.14 | async-start | bytes 18874368 | tf_op jit(solution)/shard_map/reduce_scatter | solution.py:375
  529.8 457.0 %reduce-scatter.9.cloned.1.call-start = ((), (), s32[]{:S(2)}) async-start(), calls=%async_computation.13 | async-start | bytes 18874368 | tf_op jit(solution)/shard_map/reduce_scatter | solution.py:375
  544.5 656.8 %all-gather.29.cloned.1.call-start = ((), (), s32[]{:S(2)}) async-start(), calls=%async_computation.10 | async-start | bytes 9437184 | tf_op jit(solution)/shard_map/all_gather | solution.py:382
  559.4 427.5 %copy-start.6 = (f32[256,1024]{1,0:T(8,128)S(1)}, f32[256,1024]{1,0:T(8,128)}, u32[]{:S(2)}) copy-start(f32[256,1024]{1,0:T(8,128)} %copy-done.4) | copy-start | bytes 3145732
  559.4 699.5 %all-reduce.14.cloned.1.call-start = ((), (), s32[]{:S(2)}) async-start(), calls=%async_computation.15 | async-start | bytes 12582912 | tf_op jit(solution)/shard_map/psum | solution.py:376
  1007.3 49.3 %collective-permute-start = (bf16[2,256,1024]{2,1,0:T(8,128)(2,1)S(1)}, bf16[2,256,1024]{2,1,0:T(8,128)(2,1)S(1)}, u32[]{:S(2)}, u32[]{:S(2)}) collective-permute-start(bf16[2,256,1024]{2,1,0:T(8,128)(2,1)S(1)} %get-tuple-element.86), channel_id=1, source_target_pairs={{0,4},{4,8},{8,12},{12,16},{16,20},{20,24},{24,28},{28,0},{1,5},{5... | collective-permute-start | bytes 3145736 | tf_op jit(solution)/shard_map/ppermute | solution.py:18
  1007.3 49.5 %collective-permute-start.1 = (bf16[2,256,1024]{2,1,0:T(8,128)(2,1)S(1)}, bf16[2,256,1024]{2,1,0:T(8,128)(2,1)S(1)}, u32[]{:S(2)}, u32[]{:S(2)}) collective-permute-start(bf16[2,256,1024]{2,1,0:T(8,128)(2,1)S(1)} %get-tuple-element.86), channel_id=1, source_target_pairs={{0,28},{4,0},{8,4},{12,8},{16,12},{20,16},{24,20},{28,24},{1,29},{... | collective-permute-start | bytes 3145736 | tf_op jit(solution)/shard_map/ppermute | solution.py:21
  1056.6 39.7 %collective-permute-start.2 = (bf16[2,256,1024]{2,1,0:T(8,128)(2,1)S(1)}, bf16[2,256,1024]{2,1,0:T(8,128)(2,1)}, u32[]{:S(2)}, u32[]{:S(2)}) collective-permute-start(bf16[2,256,1024]{2,1,0:T(8,128)(2,1)S(1)} %collective-permute-done), channel_id=1, source_target_pairs={{0,4},{4,8},{8,12},{12,16},{16,20},{20,24},{24,28},{28,0},{1,5},{5... | collective-permute-start | bytes 3145736 | tf_op jit(solution)/shard_map/ppermute | solution.py:18
  1056.8 48.4 %collective-permute-start.3 = (bf16[2,256,1024]{2,1,0:T(8,128)(2,1)S(1)}, bf16[2,256,1024]{2,1,0:T(8,128)(2,1)}, u32[]{:S(2)}, u32[]{:S(2)}) collective-permute-start(bf16[2,256,1024]{2,1,0:T(8,128)(2,1)S(1)} %collective-permute-done.1), channel_id=1, source_target_pairs={{0,28},{4,0},{8,4},{12,8},{16,12},{20,16},{24,20},{28,24},{1,29},{... | collective-permute-start | bytes 3145736 | tf_op jit(solution)/shard_map/ppermute | solution.py:21
  1096.2 27.8 %collective-permute-start.4 = (bf16[2,256,1024]{2,1,0:T(8,128)(2,1)}, bf16[2,256,1024]{2,1,0:T(8,128)(2,1)S(1)}, u32[]{:S(2)}, u32[]{:S(2)}) collective-permute-start(bf16[2,256,1024]{2,1,0:T(8,128)(2,1)} %collective-permute-done.2), channel_id=1, source_target_pairs={{0,4},{4,8},{8,12},{12,16},{16,20},{20,24},{24,28},{28,0},{1,5},{5... | collective-permute-start | bytes 3145736 | tf_op jit(solution)/shard_map/ppermute | solution.py:18
  1105.2 83.2 %collective-permute-start.5 = (bf16[2,256,1024]{2,1,0:T(8,128)(2,1)}, bf16[2,256,1024]{2,1,0:T(8,128)(2,1)}, u32[]{:S(2)}, u32[]{:S(2)}) collective-permute-start(bf16[2,256,1024]{2,1,0:T(8,128)(2,1)} %collective-permute-done.3), channel_id=1, source_target_pairs={{0,28},{4,0},{8,4},{12,8},{16,12},{20,16},{24,20},{28,24},{1,29},{... | collective-permute-start | bytes 3145736 | tf_op jit(solution)/shard_map/ppermute | solution.py:21
  1124.0 66.8 %collective-permute-start.6 = (bf16[2,256,1024]{2,1,0:T(8,128)(2,1)S(1)}, bf16[2,256,1024]{2,1,0:T(8,128)(2,1)}, u32[]{:S(2)}, u32[]{:S(2)}) collective-permute-start(bf16[2,256,1024]{2,1,0:T(8,128)(2,1)S(1)} %collective-permute-done.4), channel_id=1, source_target_pairs={{0,4},{4,8},{8,12},{12,16},{16,20},{20,24},{24,28},{28,0},{1,5},{5... | collective-permute-start | bytes 3145736 | tf_op jit(solution)/shard_map/ppermute | solution.py:18
  (89 other events, 3053.6 us)
Sparse Core Ops, SparseCore 0:
  9.7 84.8 all-gather.26
  96.2 80.5 all-gather.16
  178.4 63.1 all-gather.18
  243.1 27.7 all-gather.20
  272.4 81.4 all-gather.22
  355.3 80.5 all-gather.24
  470.5 48.4 reduce-scatter.6
  521.3 127.6 reduce-scatter.4
  651.3 166.6 reduce-scatter.10
  820.2 166.6 reduce-scatter.8
  989.0 125.3 all-gather.28
  1118.0 140.8 all-reduce.13
